TPU v7x, 32 devices: a whole 2x2x4 slice. The times are simulated.
32 devices in a mesh: seq: 8 (over y, x, core), tp: 4 (over z).
Axes of the slice: x: 2, y: 2, z: 4, core: 2. Of those that a mesh axis runs over, the one named last changes fastest.
Arguments:
- layer_in: bfloat16 [2, 1024, 2048], P(None, 'seq'), may hold values from -6 to 6
- positions: int32 [2, 1024], P(None, 'seq'), may hold values from 0 to 4092, as said below
- first_gain: float32 [2048], replicated, may hold values from 0.5 to 1.5
- query_proj: bfloat16 [2048, 2048], P('seq', 'tp'), may hold values from -0.125 to 0.125
- key_projection: bfloat16 [2048, 1024], P('seq', 'tp'), may hold values from -0.125 to 0.125
- value_projection: bfloat16 [2048, 1024], P('seq', 'tp'), may hold values from -0.125 to 0.125
- gate_proj: bfloat16 [2048, 2048], P('seq', 'tp'), may hold values from -0.125 to 0.125
- output_proj: bfloat16 [2048, 2048], P('tp', 'seq'), may hold values from -1.5 to 1.5
- query_gain: float32 [128], replicated, may hold values from 0.5 to 1.5
- key_norm_gain: float32 [128], replicated, may hold values from 0.5 to 1.5
- second_gain: float32 [2048], replicated, may hold values from 0.5 to 1.5
- hidden_gate: bfloat16 [2048, 6144], P('tp', 'seq'), may hold values from -0.125 to 0.125
- hidden_up: bfloat16 [2048, 6144], P('tp', 'seq'), may hold values from -0.125 to 0.125
- hidden_down: bfloat16 [6144, 2048], P('seq', 'tp'), may hold values from -0.078125 to 0.078125
- out_cotangent: bfloat16 [2, 1024, 2048], P(None, ('seq', 'tp')), may hold values from -6 to 6
Outputs:
- layer_out: bfloat16 [2, 1024, 2048], P(None, ('seq', 'tp'))
- input_grad: float32 [2, 1024, 2048], P(None, ('seq', 'tp'))
- grad_firstgain: float32 [2048], replicated
- grad_query: float32 [2048, 2048], P('seq', 'tp')
- grad_keyproj: float32 [2048, 1024], P('seq', 'tp')
- grad_valueproj: float32 [2048, 1024], P('seq', 'tp')
- grad_gating: float32 [2048, 2048], P('seq', 'tp')
- grad_outproj: float32 [2048, 2048], P('tp', 'seq')
- grad_qgain: float32 [128], replicated
- grad_kgain: float32 [128], replicated
- grad_secondgain: float32 [2048], replicated
- grad_hgate: float32 [2048, 6144], P('tp', 'seq')
- grad_hup: float32 [2048, 6144], P('tp', 'seq')
- grad_hdown: float32 [6144, 2048], P('seq', 'tp')
Inputs may be any that keep to these rules, and one draw needn't show every extreme that they name: Within each micro-batch the first token has position 0, positions rise strictly from token to token, and the last token's position is 4092.
All inputs are finite; a program needn't handle non-finite values.
Results may differ from a plain program's by a relative error of at most 0.023.
Values may be sent and summed in bfloat16 or wider, within the bound.
No kernel may reach another device: no remote copies, remote signals or barrier semaphores. Data moves between devices by JAX's collectives and lax.ppermute only.
A program may use at most 192 MiB of HBM per device.

v0:
```python
import jax
import jax.numpy as jnp
from jax import lax
from jax.sharding import PartitionSpec as P

EPS = 1e-06
ROPE_BASE = 5000000.0
NEG_LARGE = -1e30


def root_mean_square_scale(values, gain):
    return values * lax.rsqrt(jnp.mean(values * values, axis=-1, keepdims=True) + EPS) * gain


def rotate_half(values):
    middle = values.shape[-1] // 2
    return jnp.concatenate([-values[..., middle:], values[..., :middle]], axis=-1)


def rope_tables(places, head_width):
    middle = head_width // 2
    inverse = jnp.exp(
        -(jnp.arange(middle, dtype=jnp.float32) * 2.0 / head_width) * jnp.log(ROPE_BASE)
    )
    angles = places.astype(jnp.float32)[:, None] * inverse[None, :]
    cosine_table = jnp.concatenate([jnp.cos(angles), jnp.cos(angles)], axis=-1)[:, None, :]
    sine_table = jnp.concatenate([jnp.sin(angles), jnp.sin(angles)], axis=-1)[:, None, :]
    return (cosine_table, sine_table)


def apply_rotary_embedding(values, cosine_table, sine_table):
    return values * cosine_table + rotate_half(values) * sine_table


def dot_plain(left, right):
    return jnp.dot(left, right, preferred_element_type=jnp.float32)


def dot_right_t(left, right):
    return lax.dot_general(
        left, right, (((1,), (1,)), ((), ())), preferred_element_type=jnp.float32
    )


def dot_left_t(left, right):
    return lax.dot_general(
        left, right, (((0,), (0,)), ((), ())), preferred_element_type=jnp.float32
    )


def add_tuples(totals, terms):
    if totals is None:
        return terms
    return tuple((total + term for total, term in zip(totals, terms)))


def per_device(
    layer_in,
    positions,
    first_gain,
    query_proj,
    key_projection,
    value_projection,
    gate_proj,
    output_proj,
    query_gain,
    key_norm_gain,
    second_gain,
    hidden_gate,
    hidden_up,
    hidden_down,
    out_cotangent,
):
    micro_count, local_rows, model_width = layer_in.shape
    head_width = query_gain.shape[0]
    seq_count = lax.axis_size("seq")
    tp_count = lax.axis_size("tp")
    seq_place = lax.axis_index("seq")
    tp_place = lax.axis_index("tp")
    part_rows = local_rows // tp_count
    part_start = tp_place * part_rows
    total_rows = local_rows * seq_count
    block_len = min(512, total_rows)
    score_scale = head_width ** (-0.5)
    query_heads = query_proj.shape[1] // head_width
    kv_heads = key_projection.shape[1] // head_width
    query_group_size = query_heads // kv_heads
    kv_width = kv_heads * head_width
    query_pos = seq_place * local_rows + jnp.arange(local_rows, dtype=jnp.int32)
    block_total = (seq_place * local_rows + local_rows + block_len - 1) // block_len

    def layer_pass(rows_in, places, cotangent, attn_now, ffn_now):
        w_query, w_key, w_value, w_gate, w_output = attn_now
        w_hgate, w_hup, w_hdown = ffn_now
        x_rows = rows_in.astype(jnp.float32)
        cosine_table, sine_table = rope_tables(places, head_width)
        normed = root_mean_square_scale(x_rows, first_gain).astype(jnp.bfloat16)
        query_pre = dot_plain(normed, w_query)
        key_before_norm = dot_plain(normed, w_key)
        value_token_rows = dot_plain(normed, w_value).astype(jnp.bfloat16)
        gate_pre = dot_plain(normed, w_gate)

        def shape_heads(query_in, key_in, query_scale, key_scale):
            query_out = apply_rotary_embedding(
                root_mean_square_scale(
                    query_in.reshape(local_rows, query_heads, head_width), query_scale
                ),
                cosine_table,
                sine_table,
            )
            key_out = apply_rotary_embedding(
                root_mean_square_scale(key_in.reshape(local_rows, kv_heads, head_width), key_scale),
                cosine_table,
                sine_table,
            )
            return (query_out, key_out)

        (query_rot, key_rot), heads_pull = jax.vjp(
            shape_heads, query_pre, key_before_norm, query_gain, key_norm_gain
        )
        query_low = (
            query_rot.astype(jnp.bfloat16)
            .reshape(local_rows, kv_heads, query_group_size, head_width)
            .transpose(1, 2, 0, 3)
        )
        key_low = key_rot.astype(jnp.bfloat16).reshape(local_rows, kv_width)
        key_all, value_all = (
            lax.all_gather(key_low, "seq", axis=0, tiled=True),
            lax.all_gather(value_token_rows, "seq", axis=0, tiled=True),
        )

        def block_scores(row_start):
            key_block = lax.dynamic_slice_in_dim(key_all, row_start, block_len, 0).reshape(
                block_len, kv_heads, head_width
            )
            value_block = lax.dynamic_slice_in_dim(value_all, row_start, block_len, 0).reshape(
                block_len, kv_heads, head_width
            )
            scores = (
                jnp.einsum(
                    "ngid,jnd->ngij", query_low, key_block, preferred_element_type=jnp.float32
                )
                * score_scale
            )
            allowed = (row_start + jnp.arange(block_len, dtype=jnp.int32))[None, :] <= query_pos[
                :, None
            ]
            return (jnp.where(allowed, scores, NEG_LARGE), key_block, value_block)

        def stats_step(block_index, carried):
            running_max, running_sum = carried
            scores = block_scores(block_index * block_len)[0]
            new_max = jnp.maximum(running_max, jnp.max(scores, axis=-1))
            running_sum = running_sum * jnp.exp(running_max - new_max) + jnp.sum(
                jnp.exp(scores - new_max[..., None]), axis=-1
            )
            return (new_max, running_sum)

        stat_shape = (kv_heads, query_group_size, local_rows)
        running_max, running_sum = lax.fori_loop(
            0,
            block_total,
            stats_step,
            (jnp.full(stat_shape, NEG_LARGE, jnp.float32), jnp.zeros(stat_shape, jnp.float32)),
        )
        log_total = running_max + jnp.log(running_sum)

        def value_step(block_index, accum):
            scores, key_block, value_block = block_scores(block_index * block_len)
            probs_low = jnp.exp(scores - log_total[..., None]).astype(jnp.bfloat16)
            return accum + jnp.einsum(
                "ngij,jnd->ngid", probs_low, value_block, preferred_element_type=jnp.float32
            )

        attended_values = lax.fori_loop(
            0,
            block_total,
            value_step,
            jnp.zeros((kv_heads, query_group_size, local_rows, head_width), jnp.float32),
        )
        attended_values = attended_values.transpose(2, 0, 1, 3).reshape(
            local_rows, query_heads * head_width
        )
        gate_sig = jax.nn.sigmoid(gate_pre)
        gated_low = (attended_values * gate_sig).astype(jnp.bfloat16)
        branch_sum = lax.psum(dot_plain(gated_low, w_output).astype(jnp.bfloat16), "tp").astype(
            jnp.float32
        )
        middle = x_rows + branch_sum
        middle_part = lax.dynamic_slice_in_dim(middle, part_start, part_rows, 0)
        normed_two = root_mean_square_scale(middle_part, second_gain).astype(jnp.bfloat16)
        ffn_rows = lax.all_gather(normed_two, "seq", axis=0, tiled=True)
        gate_act = dot_plain(ffn_rows, w_hgate)
        upward = dot_plain(ffn_rows, w_hup)
        hidden_low = (jax.nn.silu(gate_act) * upward).astype(jnp.bfloat16)
        ffn_out = lax.psum_scatter(
            dot_plain(hidden_low, w_hdown).astype(jnp.bfloat16),
            "seq",
            scatter_dimension=0,
            tiled=True,
        ).astype(jnp.float32)
        layer_rows = (middle_part + ffn_out).astype(jnp.bfloat16)
        back_rows = lax.all_gather(cotangent, "seq", axis=0, tiled=True)
        hidden_grad = dot_right_t(back_rows, w_hdown)
        grad_hdown = dot_left_t(hidden_low, back_rows)
        gate_sigmoid = jax.nn.sigmoid(gate_act)
        gate_grad = (
            hidden_grad * upward * gate_sigmoid * (1.0 + gate_act * (1.0 - gate_sigmoid))
        ).astype(jnp.bfloat16)
        upward_grad = (hidden_grad * gate_act * gate_sigmoid).astype(jnp.bfloat16)
        grad_hgate = dot_left_t(ffn_rows, gate_grad)
        grad_hup = dot_left_t(ffn_rows, upward_grad)
        normed_two_grad = lax.psum_scatter(
            (dot_right_t(gate_grad, w_hgate) + dot_right_t(upward_grad, w_hup)).astype(
                jnp.bfloat16
            ),
            "seq",
            scatter_dimension=0,
            tiled=True,
        ).astype(jnp.float32)
        norm_two_pull = jax.vjp(root_mean_square_scale, middle_part, second_gain)[1]
        middle_from, grad_second = norm_two_pull(normed_two_grad)
        middle_grad = cotangent.astype(jnp.float32) + middle_from
        branch_grad = lax.all_gather(middle_grad.astype(jnp.bfloat16), "tp", axis=0, tiled=True)
        gated_grad = dot_right_t(branch_grad, w_output)
        grad_output = dot_left_t(gated_low, branch_grad)
        attended_grad = (gated_grad * gate_sig).astype(jnp.bfloat16)
        gate_pre_grad = (gated_grad * attended_values * gate_sig * (1.0 - gate_sig)).astype(
            jnp.bfloat16
        )
        delta = jnp.sum(
            (attended_grad.astype(jnp.float32) * attended_values).reshape(
                local_rows, kv_heads, query_group_size, head_width
            ),
            axis=-1,
        ).transpose(1, 2, 0)
        attended_grouped = attended_grad.reshape(
            local_rows, kv_heads, query_group_size, head_width
        ).transpose(1, 2, 0, 3)

        def grad_step(block_index, carried):
            query_acc, kv_acc = carried
            row_start = block_index * block_len
            scores, key_block, value_block = block_scores(row_start)
            probability = jnp.exp(scores - log_total[..., None])
            probs_grad = jnp.einsum(
                "ngid,jnd->ngij", attended_grouped, value_block, preferred_element_type=jnp.float32
            )
            scores_grad = (probability * (probs_grad - delta[..., None])).astype(jnp.bfloat16)
            query_acc = query_acc + jnp.einsum(
                "ngij,jnd->ngid", scores_grad, key_block, preferred_element_type=jnp.float32
            )
            key_piece = jnp.einsum(
                "ngij,ngid->jnd", scores_grad, query_low, preferred_element_type=jnp.float32
            )
            value_piece = jnp.einsum(
                "ngij,ngid->jnd",
                probability.astype(jnp.bfloat16),
                attended_grouped,
                preferred_element_type=jnp.float32,
            )
            update = jnp.concatenate(
                [key_piece.reshape(block_len, kv_width), value_piece.reshape(block_len, kv_width)],
                axis=1,
            )
            current = lax.dynamic_slice_in_dim(kv_acc, row_start, block_len, 0)
            return (
                query_acc,
                lax.dynamic_update_slice_in_dim(kv_acc, current + update, row_start, 0),
            )

        query_acc, kv_acc = lax.fori_loop(
            0,
            block_total,
            grad_step,
            (
                jnp.zeros((kv_heads, query_group_size, local_rows, head_width), jnp.float32),
                jnp.zeros((total_rows, 2 * kv_width), jnp.float32),
            ),
        )
        kv_grad = lax.psum_scatter(
            kv_acc.astype(jnp.bfloat16), "seq", scatter_dimension=0, tiled=True
        ).astype(jnp.float32)
        key_grad = kv_grad[:, :kv_width].reshape(local_rows, kv_heads, head_width) * score_scale
        value_low = kv_grad[:, kv_width:].astype(jnp.bfloat16)
        query_grad = (
            query_acc.transpose(2, 0, 1, 3).reshape(local_rows, query_heads, head_width)
            * score_scale
        )
        query_pre_grad, key_pre_grad, grad_qgain, grad_kgain = heads_pull((query_grad, key_grad))
        query_pre_low = query_pre_grad.astype(jnp.bfloat16)
        key_pre_low = key_pre_grad.astype(jnp.bfloat16)
        grad_query = dot_left_t(normed, query_pre_low)
        grad_keyproj = dot_left_t(normed, key_pre_low)
        grad_valueproj = dot_left_t(normed, value_low)
        grad_gating = dot_left_t(normed, gate_pre_grad)
        total = dot_right_t(query_pre_low, w_query)
        total = total + dot_right_t(key_pre_low, w_key)
        total = total + dot_right_t(value_low, w_value)
        normed_grad = lax.psum_scatter(
            (total + dot_right_t(gate_pre_grad, w_gate)).astype(jnp.bfloat16),
            "tp",
            scatter_dimension=0,
            tiled=True,
        ).astype(jnp.float32)
        x_part = lax.dynamic_slice_in_dim(x_rows, part_start, part_rows, 0)
        norm_one_pull = jax.vjp(root_mean_square_scale, x_part, first_gain)[1]
        input_from, grad_first = norm_one_pull(normed_grad)
        input_grad = middle_grad + input_from
        return (
            layer_rows,
            input_grad,
            (grad_query, grad_keyproj, grad_valueproj, grad_gating, grad_output),
            (grad_hgate, grad_hup, grad_hdown),
            (grad_first, grad_qgain, grad_kgain, grad_second),
        )

    outputs_list = []
    input_list = []
    attn_total = None
    ffn_total = None
    gain_total = None
    for micro_index in range(micro_count):
        attn_now = (
            lax.all_gather(query_proj, "seq", axis=0, tiled=True),
            lax.all_gather(key_projection, "seq", axis=0, tiled=True),
            lax.all_gather(value_projection, "seq", axis=0, tiled=True),
            lax.all_gather(gate_proj, "seq", axis=0, tiled=True),
            lax.all_gather(output_proj, "seq", axis=1, tiled=True),
        )
        ffn_now = (
            lax.all_gather(hidden_gate, "tp", axis=0, tiled=True),
            lax.all_gather(hidden_up, "tp", axis=0, tiled=True),
            lax.all_gather(hidden_down, "tp", axis=1, tiled=True),
        )
        layer_rows, input_grad, attn_grads, ffn_grads, gain_grads = layer_pass(
            layer_in[micro_index],
            positions[micro_index],
            out_cotangent[micro_index],
            attn_now,
            ffn_now,
        )
        attn_grads = (
            lax.psum_scatter(
                attn_grads[0].astype(jnp.bfloat16), "seq", scatter_dimension=0, tiled=True
            ).astype(jnp.float32),
            lax.psum_scatter(
                attn_grads[1].astype(jnp.bfloat16), "seq", scatter_dimension=0, tiled=True
            ).astype(jnp.float32),
            lax.psum_scatter(
                attn_grads[2].astype(jnp.bfloat16), "seq", scatter_dimension=0, tiled=True
            ).astype(jnp.float32),
            lax.psum_scatter(
                attn_grads[3].astype(jnp.bfloat16), "seq", scatter_dimension=0, tiled=True
            ).astype(jnp.float32),
            lax.psum_scatter(
                attn_grads[4].astype(jnp.bfloat16), "seq", scatter_dimension=1, tiled=True
            ).astype(jnp.float32),
        )
        ffn_grads = (
            lax.psum_scatter(
                ffn_grads[0].astype(jnp.bfloat16), "tp", scatter_dimension=0, tiled=True
            ).astype(jnp.float32),
            lax.psum_scatter(
                ffn_grads[1].astype(jnp.bfloat16), "tp", scatter_dimension=0, tiled=True
            ).astype(jnp.float32),
            lax.psum_scatter(
                ffn_grads[2].astype(jnp.bfloat16), "tp", scatter_dimension=1, tiled=True
            ).astype(jnp.float32),
        )
        attn_total = add_tuples(attn_total, attn_grads)
        ffn_total = add_tuples(ffn_total, ffn_grads)
        gain_total = add_tuples(gain_total, gain_grads)
        outputs_list.append(layer_rows)
        input_list.append(input_grad)
    gains_summed = lax.psum(
        (gain_total[0], gain_total[1], gain_total[2], gain_total[3]), ("seq", "tp")
    )
    return (
        jnp.stack(outputs_list),
        jnp.stack(input_list),
        gains_summed[0],
        attn_total[0],
        attn_total[1],
        attn_total[2],
        attn_total[3],
        attn_total[4],
        gains_summed[1],
        gains_summed[2],
        gains_summed[3],
        ffn_total[0],
        ffn_total[1],
        ffn_total[2],
    )


def solution(mesh):
    in_specs = (
        P(None, "seq", None),
        P(None, "seq"),
        P(),
        P("seq", "tp"),
        P("seq", "tp"),
        P("seq", "tp"),
        P("seq", "tp"),
        P("tp", "seq"),
        P(),
        P(),
        P(),
        P("tp", "seq"),
        P("tp", "seq"),
        P("seq", "tp"),
        P(None, ("seq", "tp"), None),
    )
    out_specs = (
        P(None, ("seq", "tp"), None),
        P(None, ("seq", "tp"), None),
        P(),
        P("seq", "tp"),
        P("seq", "tp"),
        P("seq", "tp"),
        P("seq", "tp"),
        P("tp", "seq"),
        P(),
        P(),
        P(),
        P("tp", "seq"),
        P("tp", "seq"),
        P("seq", "tp"),
    )
    return jax.shard_map(
        per_device, mesh=mesh, in_specs=in_specs, out_specs=out_specs, check_vma=False
    )
```

profile of v0, /device:TPU:0, one launch (start us, length us, event | category | flops | bytes accessed | tf_op | source)
XLA Modules:
  0.0 1661.5 jit_solution(12021355305150409271)
XLA Ops:
  13.9 22.1 %all-gather.15.cloned.1.call-done = bf16[2048,256]{1,0:T(8,128)(2,1)} async-done(((bf16[256,256]{1,0:T(8,128)(2,1)}), bf16[2048,256]{1,0:T(8,128)(2,1)}) %all-gather.15.cloned.1.call-update) | async-done | bytes 1048592 | tf_op jit(solution)/shard_map/all_gather | solution.py:326
  126.4 25.0 %all-gather.23.cloned.1.call-done = bf16[512,2048]{1,0:T(8,128)(2,1)} async-done(((bf16[512,256]{1,0:T(8,128)(2,1)}), bf16[512,2048]{1,0:T(8,128)(2,1)}) %all-gather.23.cloned.1.call-update) | async-done | bytes 2097168 | tf_op jit(solution)/shard_map/all_gather | solution.py:329
  159.9 47.8 %all-reduce.12.cloned.1.call-done = (bf16[128,2048]{1,0:T(8,128)(2,1)}, bf16[128,2048]{1,0:T(8,128)(2,1)}) async-done(((bf16[128,2048]{1,0:T(8,128)(2,1)}, bf16[128,2048]{1,0:T(8,128)(2,1)}), (bf16[128,2048]{1,0:T(8,128)(2,1)}, bf16[128,2048]{1,0:T(8,128)(2,1)})) %all-reduce.12.cloned.1.call-update) | async-done | bytes 1048592 | tf_op jit(solution)/shard_map/psum | solution.py:186
  213.0 59.0 %all-gather.27.cloned.1.call-done = bf16[2048,768]{1,0:T(8,128)(2,1)} async-done(((bf16[512,768]{1,0:T(8,128)(2,1)}), bf16[2048,768]{1,0:T(8,128)(2,1)}) %all-gather.27.cloned.1.call-update) | async-done | bytes 3145744 | tf_op jit(solution)/shard_map/all_gather | solution.py:332
  272.0 24.5 %all-gather.25.cloned.1.call-done = bf16[256,2048]{1,0:T(8,128)(2,1)} async-done(((bf16[32,2048]{1,0:T(8,128)(2,1)}), bf16[256,2048]{1,0:T(8,128)(2,1)}) %all-gather.25.cloned.1.call-update) | async-done | bytes 1048592 | tf_op jit(solution)/shard_map/all_gather | solution.py:192
  300.6 61.0 %all-gather.29.cloned.1.call-done = bf16[2048,768]{1,0:T(8,128)(2,1)} async-done(((bf16[512,768]{1,0:T(8,128)(2,1)}), bf16[2048,768]{1,0:T(8,128)(2,1)}) %all-gather.29.cloned.1.call-update) | async-done | bytes 3145744 | tf_op jit(solution)/shard_map/all_gather | solution.py:333
  365.6 19.7 %all-gather.35.cloned.1.call-done = bf16[1,256,2048]{2,1,0:T(8,128)(2,1)} async-done(((bf16[1,32,2048]{2,1,0:T(8,128)(2,1)}), bf16[1,256,2048]{2,1,0:T(8,128)(2,1)}) %all-gather.35.cloned.1.call-update) | async-done | bytes 1048592 | tf_op jit(solution)/shard_map/all_gather | solution.py:203
  385.4 65.0 %all-gather.31.cloned.1.call-done = bf16[768,2048]{1,0:T(8,128)(2,1)} async-done(((bf16[768,512]{1,0:T(8,128)(2,1)}), bf16[768,2048]{1,0:T(8,128)(2,1)}) %all-gather.31.cloned.1.call-update) | async-done | bytes 3145744 | tf_op jit(solution)/shard_map/all_gather | solution.py:334
  461.9 32.3 %reduce-scatter.33.cloned.1.call-done = bf16[32,2048]{1,0:T(8,128)(2,1)} async-done(((bf16[256,2048]{1,0:T(8,128)(2,1)}), bf16[32,2048]{1,0:T(8,128)(2,1)}) %reduce-scatter.33.cloned.1.call-update) | async-done | bytes 131088 | tf_op jit(solution)/shard_map/reduce_scatter | solution.py:213
  497.8 15.4 all_gather.77
  526.6 38.5 %reduce-scatter.73.cloned.1.call-done = bf16[128,512]{1,0:T(8,128)(2,1)} async-done(((bf16[1024,512]{1,0:T(8,128)(2,1)}), bf16[128,512]{1,0:T(8,128)(2,1)}) %reduce-scatter.73.cloned.1.call-update) | async-done | bytes 131088
  594.8 20.7 %all-gather.37.cloned.1.call-done = bf16[1,256,2048]{2,1,0:T(8,128)(2,1)} async-done(((bf16[1,32,2048]{2,1,0:T(8,128)(2,1)}), bf16[1,256,2048]{2,1,0:T(8,128)(2,1)}) %all-gather.37.cloned.1.call-update) | async-done | bytes 1048592 | tf_op jit(solution)/shard_map/all_gather | solution.py:203
  642.9 35.0 %reduce-scatter.37.cloned.1.call-done = bf16[32,2048]{1,0:T(8,128)(2,1)} async-done(((bf16[256,2048]{1,0:T(8,128)(2,1)}), bf16[32,2048]{1,0:T(8,128)(2,1)}) %reduce-scatter.37.cloned.1.call-update) | async-done | bytes 131088 | tf_op jit(solution)/shard_map/reduce_scatter | solution.py:213
  680.7 36.2 %reduce-scatter.29.cloned.1.call-done = bf16[32,2048]{1,0:T(8,128)(2,1)} async-done(((bf16[256,2048]{1,0:T(8,128)(2,1)}), bf16[32,2048]{1,0:T(8,128)(2,1)}) %reduce-scatter.29.cloned.1.call-update) | async-done | bytes 131088 | tf_op jit(solution)/shard_map/reduce_scatter | solution.py:196
  716.9 39.7 %reduce-scatter.31.cloned.1.call-done = bf16[32,2048]{1,0:T(8,128)(2,1)} async-done(((bf16[256,2048]{1,0:T(8,128)(2,1)}), bf16[32,2048]{1,0:T(8,128)(2,1)}) %reduce-scatter.31.cloned.1.call-update) | async-done | bytes 131088 | tf_op jit(solution)/shard_map/reduce_scatter | solution.py:196
  759.0 15.4 all_gather.79
  785.4 39.4 %reduce-scatter.75.cloned.1.call-done = bf16[128,512]{1,0:T(8,128)(2,1)} async-done(((bf16[1024,512]{1,0:T(8,128)(2,1)}), bf16[128,512]{1,0:T(8,128)(2,1)}) %reduce-scatter.75.cloned.1.call-update) | async-done | bytes 131088
  876.7 39.7 %all-reduce.8 = (f32[2048]{0:T(1024)}, f32[128]{0:T(128)}, f32[128]{0:T(128)}, f32[2048]{0:T(1024)}) all-reduce(f32[2048]{0:T(1024)S(1)} %add.486, f32[128]{0:T(128)S(1)} %add.492, f32[128]{0:T(128)S(1)} %add.493, f32[2048]{0:T(1024)S(1)} %add.494), channel_id=1, replica_groups=mesh['seq'=8,'tp'=4] {'seq','tp'}, use_global_device_ids=true, to_apply=%region_48.49 | all-reduce | flops 4352 | bytes 34816 | tf_op jit(solution)/shard_map/psum | solution.py:376
  932.7 37.4 %reduce-scatter.49.cloned.1.call-done = bf16[256,256]{1,0:T(8,128)(2,1)} async-done(((bf16[2048,256]{1,0:T(8,128)(2,1)}), bf16[256,256]{1,0:T(8,128)(2,1)}) %reduce-scatter.49.cloned.1.call-update) | async-done | bytes 131088 | tf_op jit(solution)/shard_map/reduce_scatter | solution.py:350
  970.0 39.7 %reduce-scatter.51.cloned.1.call-done = bf16[256,256]{1,0:T(8,128)(2,1)} async-done(((bf16[2048,256]{1,0:T(8,128)(2,1)}), bf16[256,256]{1,0:T(8,128)(2,1)}) %reduce-scatter.51.cloned.1.call-update) | async-done | bytes 131088 | tf_op jit(solution)/shard_map/reduce_scatter | solution.py:350
  1011.5 42.6 %reduce-scatter.41.cloned.1.call-done = bf16[256,512]{1,0:T(8,128)(2,1)} async-done(((bf16[2048,512]{1,0:T(8,128)(2,1)}), bf16[256,512]{1,0:T(8,128)(2,1)}) %reduce-scatter.41.cloned.1.call-update) | async-done | bytes 262160 | tf_op jit(solution)/shard_map/reduce_scatter | solution.py:344
  1054.0 44.3 %reduce-scatter.43.cloned.1.call-done = bf16[256,512]{1,0:T(8,128)(2,1)} async-done(((bf16[2048,512]{1,0:T(8,128)(2,1)}), bf16[256,512]{1,0:T(8,128)(2,1)}) %reduce-scatter.43.cloned.1.call-update) | async-done | bytes 262160 | tf_op jit(solution)/shard_map/reduce_scatter | solution.py:344
  1100.2 42.5 %reduce-scatter.53.cloned.1.call-done = bf16[256,512]{1,0:T(8,128)(2,1)} async-done(((bf16[2048,512]{1,0:T(8,128)(2,1)}), bf16[256,512]{1,0:T(8,128)(2,1)}) %reduce-scatter.53.cloned.1.call-update) | async-done | bytes 262160 | tf_op jit(solution)/shard_map/reduce_scatter | solution.py:353
  1142.8 44.4 %reduce-scatter.55.cloned.1.call-done = bf16[256,512]{1,0:T(8,128)(2,1)} async-done(((bf16[2048,512]{1,0:T(8,128)(2,1)}), bf16[256,512]{1,0:T(8,128)(2,1)}) %reduce-scatter.55.cloned.1.call-update) | async-done | bytes 262160 | tf_op jit(solution)/shard_map/reduce_scatter | solution.py:353
  1189.1 42.4 %reduce-scatter.57.cloned.1.call-done = bf16[512,256]{1,0:T(8,128)(2,1)} async-done(((bf16[512,2048]{1,0:T(8,128)(2,1)}), bf16[512,256]{1,0:T(8,128)(2,1)}) %reduce-scatter.57.cloned.1.call-update) | async-done | bytes 262160 | tf_op jit(solution)/shard_map/reduce_scatter | solution.py:356
  1231.5 44.4 %reduce-scatter.59.cloned.1.call-done = bf16[512,256]{1,0:T(8,128)(2,1)} async-done(((bf16[512,2048]{1,0:T(8,128)(2,1)}), bf16[512,256]{1,0:T(8,128)(2,1)}) %reduce-scatter.59.cloned.1.call-update) | async-done | bytes 262160 | tf_op jit(solution)/shard_map/reduce_scatter | solution.py:356
  1277.8 60.9 %reduce-scatter.61.cloned.1.call-done = bf16[512,768]{1,0:T(8,128)(2,1)} async-done(((bf16[2048,768]{1,0:T(8,128)(2,1)}), bf16[512,768]{1,0:T(8,128)(2,1)}) %reduce-scatter.61.cloned.1.call-update) | async-done | bytes 786448 | tf_op jit(solution)/shard_map/reduce_scatter | solution.py:361
  1338.7 62.5 %reduce-scatter.63.cloned.1.call-done = bf16[512,768]{1,0:T(8,128)(2,1)} async-done(((bf16[2048,768]{1,0:T(8,128)(2,1)}), bf16[512,768]{1,0:T(8,128)(2,1)}) %reduce-scatter.63.cloned.1.call-update) | async-done | bytes 786448 | tf_op jit(solution)/shard_map/reduce_scatter | solution.py:361
  1403.9 60.0 %reduce-scatter.65.cloned.1.call-done = bf16[512,768]{1,0:T(8,128)(2,1)} async-done(((bf16[2048,768]{1,0:T(8,128)(2,1)}), bf16[512,768]{1,0:T(8,128)(2,1)}) %reduce-scatter.65.cloned.1.call-update) | async-done | bytes 786448 | tf_op jit(solution)/shard_map/reduce_scatter | solution.py:364
  1463.8 62.6 %reduce-scatter.67.cloned.1.call-done = bf16[512,768]{1,0:T(8,128)(2,1)} async-done(((bf16[2048,768]{1,0:T(8,128)(2,1)}), bf16[512,768]{1,0:T(8,128)(2,1)}) %reduce-scatter.67.cloned.1.call-update) | async-done | bytes 786448 | tf_op jit(solution)/shard_map/reduce_scatter | solution.py:364
  1529.2 59.8 %reduce-scatter.69.cloned.1.call-done = bf16[768,512]{1,0:T(8,128)(2,1)} async-done(((bf16[768,2048]{1,0:T(8,128)(2,1)}), bf16[768,512]{1,0:T(8,128)(2,1)}) %reduce-scatter.69.cloned.1.call-update) | async-done | bytes 786448 | tf_op jit(solution)/shard_map/reduce_scatter | solution.py:367
  1589.0 62.5 %reduce-scatter.71.cloned.1.call-done = bf16[768,512]{1,0:T(8,128)(2,1)} async-done(((bf16[768,2048]{1,0:T(8,128)(2,1)}), bf16[768,512]{1,0:T(8,128)(2,1)}) %reduce-scatter.71.cloned.1.call-update) | async-done | bytes 786448 | tf_op jit(solution)/shard_map/reduce_scatter | solution.py:367
  (570 shorter events, 317.1 us)
Async XLA Ops:
  9.4 112.7 %all-gather.21.cloned.1.call-start = ((), (), s32[]{:S(2)}) async-start(), calls=%async_computation.27 | async-start | bytes 2359296 | tf_op jit(solution)/shard_map/all_gather | solution.py:328
  10.0 141.4 %all-gather.23.cloned.1.call-start = ((), (), s32[]{:S(2)}) async-start(), calls=%async_computation.28 | async-start | bytes 2359296 | tf_op jit(solution)/shard_map/all_gather | solution.py:329
  10.6 197.2 %all-reduce.12.cloned.1.call-start = ((), (), s32[]{:S(2)}) async-start(), calls=%async_computation.60 | async-start | bytes 2097152 | tf_op jit(solution)/shard_map/psum | solution.py:186
  155.6 116.4 %all-gather.27.cloned.1.call-start = ((), (), s32[]{:S(2)}) async-start(), calls=%async_computation.30 | async-start | bytes 3932160 | tf_op jit(solution)/shard_map/all_gather | solution.py:332
  156.4 140.1 %all-gather.25.cloned.1.call-start = ((), (), s32[]{:S(2)}) async-start(), calls=%async_computation.29 | async-start | bytes 1179648 | tf_op jit(solution)/shard_map/all_gather | solution.py:192
  209.7 151.9 %all-gather.29.cloned.1.call-start = ((), (), s32[]{:S(2)}) async-start(), calls=%async_computation.31 | async-start | bytes 3932160 | tf_op jit(solution)/shard_map/all_gather | solution.py:333
  210.5 174.9 %all-gather.35.cloned.1.call-start = ((), (), s32[]{:S(2)}) async-start(), calls=%async_computation.56 | async-start | bytes 1179648 | tf_op jit(solution)/shard_map/all_gather | solution.py:203
  212.2 238.2 %all-gather.31.cloned.1.call-start = ((), (), s32[]{:S(2)}) async-start(), calls=%async_computation.32 | async-start | bytes 3932160 | tf_op jit(solution)/shard_map/all_gather | solution.py:334
  213.0 281.2 %reduce-scatter.33.cloned.1.call-start = ((), (), s32[]{:S(2)}) async-start(), calls=%async_computation.36 | async-start | bytes 1179648 | tf_op jit(solution)/shard_map/reduce_scatter | solution.py:213
  459.4 105.8 %reduce-scatter.73.cloned.1.call-start = ((), (), s32[]{:S(2)}) async-start(), calls=%async_computation.58 | async-start | bytes 1179648
  524.7 90.8 %all-gather.37.cloned.1.call-start = ((), (), s32[]{:S(2)}) async-start(), calls=%async_computation.57 | async-start | bytes 1179648 | tf_op jit(solution)/shard_map/all_gather | solution.py:203
  525.3 114.8 %reduce-scatter.35.cloned.1.call-start = ((), (), s32[]{:S(2)}) async-start(), calls=%async_computation.37 | async-start | bytes 655360 | tf_op jit(solution)/shard_map/reduce_scatter | solution.py:300
  575.1 102.8 %reduce-scatter.37.cloned.1.call-start = ((), (), s32[]{:S(2)}) async-start(), calls=%async_computation.38 | async-start | bytes 1179648 | tf_op jit(solution)/shard_map/reduce_scatter | solution.py:213
  623.4 93.5 %reduce-scatter.29.cloned.1.call-start = ((), (), s32[]{:S(2)}) async-start(), calls=%async_computation.33 | async-start | bytes 1179648 | tf_op jit(solution)/shard_map/reduce_scatter | solution.py:196
  627.4 129.3 %reduce-scatter.31.cloned.1.call-start = ((), (), s32[]{:S(2)}) async-start(), calls=%async_computation.35 | async-start | bytes 1179648 | tf_op jit(solution)/shard_map/reduce_scatter | solution.py:196
  631.4 193.3 %reduce-scatter.75.cloned.1.call-start = ((), (), s32[]{:S(2)}) async-start(), calls=%async_computation.59 | async-start | bytes 1179648
  784.6 91.0 %reduce-scatter.39.cloned.1.call-start = ((), (), s32[]{:S(2)}) async-start(), calls=%async_computation.39 | async-start | bytes 655360 | tf_op jit(solution)/shard_map/reduce_scatter | solution.py:300
  832.9 98.1 %reduce-scatter.47.cloned.1.call-start = ((), (), s32[]{:S(2)}) async-start(), calls=%async_computation.43 | async-start | bytes 1179648 | tf_op jit(solution)/shard_map/reduce_scatter | solution.py:347
  834.5 135.5 %reduce-scatter.49.cloned.1.call-start = ((), (), s32[]{:S(2)}) async-start(), calls=%async_computation.44 | async-start | bytes 1179648 | tf_op jit(solution)/shard_map/reduce_scatter | solution.py:350
  836.1 173.7 %reduce-scatter.51.cloned.1.call-start = ((), (), s32[]{:S(2)}) async-start(), calls=%async_computation.45 | async-start | bytes 1179648 | tf_op jit(solution)/shard_map/reduce_scatter | solution.py:350
  837.7 216.3 %reduce-scatter.41.cloned.1.call-start = ((), (), s32[]{:S(2)}) async-start(), calls=%async_computation.40 | async-start | bytes 2359296 | tf_op jit(solution)/shard_map/reduce_scatter | solution.py:344
  839.9 258.4 %reduce-scatter.43.cloned.1.call-start = ((), (), s32[]{:S(2)}) async-start(), calls=%async_computation.41 | async-start | bytes 2359296 | tf_op jit(solution)/shard_map/reduce_scatter | solution.py:344
  842.2 300.5 %reduce-scatter.53.cloned.1.call-start = ((), (), s32[]{:S(2)}) async-start(), calls=%async_computation.46 | async-start | bytes 2359296 | tf_op jit(solution)/shard_map/reduce_scatter | solution.py:353
  844.5 342.7 %reduce-scatter.55.cloned.1.call-start = ((), (), s32[]{:S(2)}) async-start(), calls=%async_computation.47 | async-start | bytes 2359296 | tf_op jit(solution)/shard_map/reduce_scatter | solution.py:353
  846.7 384.8 %reduce-scatter.57.cloned.1.call-start = ((), (), s32[]{:S(2)}) async-start(), calls=%async_computation.48 | async-start | bytes 2359296 | tf_op jit(solution)/shard_map/reduce_scatter | solution.py:356
  848.9 427.0 %reduce-scatter.59.cloned.1.call-start = ((), (), s32[]{:S(2)}) async-start(), calls=%async_computation.49 | async-start | bytes 2359296 | tf_op jit(solution)/shard_map/reduce_scatter | solution.py:356
  851.0 487.6 %reduce-scatter.61.cloned.1.call-start = ((), (), s32[]{:S(2)}) async-start(), calls=%async_computation.50 | async-start | bytes 3932160 | tf_op jit(solution)/shard_map/reduce_scatter | solution.py:361
  853.9 547.3 %reduce-scatter.63.cloned.1.call-start = ((), (), s32[]{:S(2)}) async-start(), calls=%async_computation.51 | async-start | bytes 3932160 | tf_op jit(solution)/shard_map/reduce_scatter | solution.py:361
  857.9 606.0 %reduce-scatter.65.cloned.1.call-start = ((), (), s32[]{:S(2)}) async-start(), calls=%async_computation.52 | async-start | bytes 3932160 | tf_op jit(solution)/shard_map/reduce_scatter | solution.py:364
  861.7 664.8 %reduce-scatter.67.cloned.1.call-start = ((), (), s32[]{:S(2)}) async-start(), calls=%async_computation.53 | async-start | bytes 3932160 | tf_op jit(solution)/shard_map/reduce_scatter | solution.py:364
  865.4 723.5 %reduce-scatter.69.cloned.1.call-start = ((), (), s32[]{:S(2)}) async-start(), calls=%async_computation.54 | async-start | bytes 3932160 | tf_op jit(solution)/shard_map/reduce_scatter | solution.py:367
  869.5 782.0 %reduce-scatter.71.cloned.1.call-start = ((), (), s32[]{:S(2)}) async-start(), calls=%async_computation.55 | async-start | bytes 3932160 | tf_op jit(solution)/shard_map/reduce_scatter | solution.py:367
  (138 other events, 3055.5 us)
Sparse Core Ops, SparseCore 0:
  9.9 26.0 all-gather.14
  37.9 23.6 all-gather.18
  63.5 28.4 all-gather.16
  93.7 27.7 all-gather.20
  123.3 28.0 all-gather.22
  155.8 51.9 all-reduce.11
  209.3 62.6 all-gather.26
  298.1 63.4 all-gather.28
  386.9 63.4 all-gather.30
  459.5 34.6 reduce-scatter.32
  524.2 40.9 reduce-scatter.72
  566.9 23.3 all-gather.32
  643.6 34.2 reduce-scatter.36
  680.9 35.9 reduce-scatter.28
  720.7 35.9 reduce-scatter.30
  784.7 39.9 reduce-scatter.74
  857.0 34.1 reduce-scatter.44
  895.0 35.9 reduce-scatter.46
  934.0 35.9 reduce-scatter.48
  973.8 35.9 reduce-scatter.50
  1012.9 41.0 reduce-scatter.40
  1057.2 41.1 reduce-scatter.42
  1101.6 41.1 reduce-scatter.52
  1146.0 41.1 reduce-scatter.54
  1190.3 41.1 reduce-scatter.56
  1234.8 41.0 reduce-scatter.58
  1278.2 60.4 reduce-scatter.60
  1340.8 60.3 reduce-scatter.62
  1403.5 60.3 reduce-scatter.64
  1466.1 60.3 reduce-scatter.66
  1528.6 60.3 reduce-scatter.68
  1591.1 60.3 reduce-scatter.70
  (5 shorter events, 110.7 us)
where the time goes:
time: 1670 us; the launch traced here: 1660 us
  waiting for transfers between devices  1320 us (79%)
  blocking collectives  111 us (7%)
  matrix products  108 us (6%)
  other arithmetic  59 us (4%)
  local copies, waits for them, and re-layouts  38.3 us (2%)
  between operations  16.9 us (1%)
    reduce_scatter x2, waiting for transfers between devices, per_device(): lax.psum_scatter(ffn_grads[0].astype(jnp.bfloat16), 'tp', scatter_dimensi...  123 us
    reduce_scatter x2, waiting for transfers between devices, per_device(): lax.psum_scatter(ffn_grads[1].astype(jnp.bfloat16), 'tp', scatter_dimensi...  123 us
    reduce_scatter x2, waiting for transfers between devices, per_device(): lax.psum_scatter(ffn_grads[2].astype(jnp.bfloat16), 'tp', scatter_dimensi...  122 us
    reduce_scatter x2, waiting for transfers between devices, per_device(): lax.psum_scatter(attn_grads[3].astype(jnp.bfloat16), 'seq', scatter_dimen...  87 us
    reduce_scatter x2, waiting for transfers between devices, per_device(): lax.psum_scatter(attn_grads[0].astype(jnp.bfloat16), 'seq', scatter_dimen...  86.9 us
    reduce_scatter x2, waiting for transfers between devices, per_device(): lax.psum_scatter(attn_grads[4].astype(jnp.bfloat16), 'seq', scatter_dimen...  86.8 us
    unnamed x39, waiting for transfers between devices  84.6 us
    reduce_scatter x2, waiting for transfers between devices, per_device(): lax.psum_scatter(attn_grads[2].astype(jnp.bfloat16), 'seq', scatter_dimen...  77.1 us
  transfers between devices with their start and end apart: 37, of which 33 were waited for; matrix products, arithmetic and copies ran while one was open for 9% of the time, Pallas kernels for 0%

commit v1 on v0

v1 whole, which is shorter than its diff:
```python
import jax
import jax.numpy as jnp
from jax import lax
from jax.sharding import PartitionSpec as P

EPS = 1e-06
ROPE_BASE = 5000000.0
NEG_LARGE = -1e30
F32 = jnp.float32
LOW = jnp.bfloat16


def root_mean_square_scale(values, gain):
    return values * lax.rsqrt(jnp.mean(values * values, axis=-1, keepdims=True) + EPS) * gain


def rotate_half(values):
    middle = values.shape[-1] // 2
    return jnp.concatenate([-values[..., middle:], values[..., :middle]], axis=-1)


def rope_tables(places, head_width):
    middle = head_width // 2
    inverse = jnp.exp(-(jnp.arange(middle, dtype=F32) * 2.0 / head_width) * jnp.log(ROPE_BASE))
    angles = places.astype(F32)[:, None] * inverse[None, :]
    cosine_table = jnp.concatenate([jnp.cos(angles), jnp.cos(angles)], axis=-1)[:, None, :]
    sine_table = jnp.concatenate([jnp.sin(angles), jnp.sin(angles)], axis=-1)[:, None, :]
    return (cosine_table, sine_table)


def apply_rotary_embedding(values, cosine_table, sine_table):
    return values * cosine_table + rotate_half(values) * sine_table


def dot_nn(left, right):
    return jnp.dot(left, right, preferred_element_type=F32)


def dot_nt(left, right):
    return lax.dot_general(left, right, (((1,), (1,)), ((), ())), preferred_element_type=F32)


def dot_tn(left, right):
    return lax.dot_general(left, right, (((0,), (0,)), ((), ())), preferred_element_type=F32)


def swap(value, axis, mask):
    count = lax.axis_size(axis)
    return lax.ppermute(value, axis, [(i, i ^ mask) for i in range(count)])


def gather_slots(value, axis, order):
    have = {0: value}
    for mask in order:
        have.update({s ^ mask: swap(v, axis, mask) for s, v in have.items()})
    return [have[s] for s in range(len(have))]


def scatter_slots(pieces, axis, order):
    now = dict(enumerate(pieces))
    for mask in order:
        now = {
            s: v.astype(F32) + swap(now[s ^ mask].astype(LOW), axis, mask).astype(F32)
            for s, v in now.items()
            if not s & mask
        }
    return now[0]


def spread_tp(value):
    count = lax.axis_size("tp")
    return [value] + [swap(value, "tp", k) for k in range(1, count)]


def tree_sum(terms):
    while len(terms) > 1:
        terms = [terms[i] + terms[i + 1] for i in range(0, len(terms), 2)]
    return terms[0]


def collect_tp(rows):
    count = lax.axis_size("tp")
    blocks = rows.reshape(count, rows.shape[0] // count, rows.shape[1])
    got = [blocks[0]]
    got += [swap(blocks[k].astype(LOW), "tp", k).astype(F32) for k in range(1, count)]
    return tree_sum(got)


def per_device(
    layer_in,
    positions,
    first_gain,
    query_proj,
    key_projection,
    value_projection,
    gate_proj,
    output_proj,
    query_gain,
    key_norm_gain,
    second_gain,
    hidden_gate,
    hidden_up,
    hidden_down,
    out_cotangent,
):
    micros, local_rows, width = layer_in.shape
    head = query_gain.shape[0]
    n = lax.axis_size("seq")
    p = lax.axis_size("tp")
    me_seq = lax.axis_index("seq")
    me_tp = lax.axis_index("tp")
    part = local_rows // p
    tokens = micros * local_rows
    ptok = micros * part
    block = width // n
    chunk = width // p
    q_width = query_proj.shape[1]
    kv_width = key_projection.shape[1]
    q_heads = q_width // head
    kv_heads = kv_width // head
    group = q_heads // kv_heads
    units = hidden_down.shape[0] // p
    total_rows = local_rows * n
    scale = head ** (-0.5)
    masks = [1 << b for b in range((n - 1).bit_length())]
    go_a = masks[1:] + masks[:1]
    go_b = masks[:0:-1] + masks[:1]
    back_a = masks[:1] + masks[1:]
    back_b = masks[:1] + masks[:0:-1]

    def permute_columns(value):
        return jnp.concatenate(
            [
                lax.dynamic_slice_in_dim(value, (me_seq ^ j) * block, block, value.ndim - 1)
                for j in range(n)
            ],
            axis=-1,
        )

    def token_slots(value):
        return jnp.stack(
            [lax.dynamic_slice_in_dim(value, (me_tp ^ k) * part, part, 1) for k in range(p)]
        )

    w_q = gather_slots(query_proj, "seq", go_a)
    w_kv = gather_slots(
        jnp.concatenate([key_projection, value_projection], axis=1), "seq", go_b
    )
    w_g = gather_slots(gate_proj, "seq", go_a)
    w_o = gather_slots(output_proj.T, "seq", go_b)

    def fetch_units(weight):
        blocks = weight.reshape(p, units, chunk)
        result = jnp.zeros((units, width), LOW)
        for k in range(p):
            piece = lax.dynamic_index_in_dim(blocks, me_tp ^ k, 0, keepdims=False)
            if k:
                piece = swap(piece, "tp", k)
            result = lax.dynamic_update_slice_in_dim(result, piece, (me_tp ^ k) * chunk, 1)
        return result

    half = units // 2
    f_gate = gather_slots(fetch_units(hidden_gate.T), "seq", go_a)
    f_up = gather_slots(fetch_units(hidden_up.T), "seq", go_b)
    down_own = fetch_units(hidden_down)
    f_down_a = gather_slots(down_own[:half], "seq", go_a)
    f_down_b = gather_slots(down_own[half:], "seq", go_b)
    f_gate = jnp.concatenate(f_gate)
    f_up = jnp.concatenate(f_up)
    f_down = jnp.concatenate([v for pair in zip(f_down_a, f_down_b) for v in pair])

    cot_part = out_cotangent.reshape(ptok, width)
    cot = jnp.concatenate(spread_tp(cot_part))

    x_slots = token_slots(layer_in)
    x_part = x_slots[0].reshape(ptok, width).astype(F32)
    x_perm = permute_columns(x_slots.reshape(tokens, width)).astype(F32)
    places = token_slots(positions).reshape(tokens)
    gain_perm = permute_columns(first_gain)
    cosine_table, sine_table = rope_tables(places, head)
    normed = root_mean_square_scale(x_perm, gain_perm).astype(LOW)
    w_q = jnp.concatenate(w_q)
    w_kv = jnp.concatenate(w_kv)
    w_g = jnp.concatenate(w_g)
    w_o = jnp.concatenate(w_o)
    query_pre = dot_nn(normed, w_q)
    kv_pre = dot_nn(normed, w_kv)
    key_pre = kv_pre[:, :kv_width]
    value_low = kv_pre[:, kv_width:].astype(LOW)
    gate_pre = dot_nn(normed, w_g)

    def shape_heads(query_in, key_in, query_scale, key_scale):
        query_out = apply_rotary_embedding(
            root_mean_square_scale(query_in.reshape(tokens, q_heads, head), query_scale),
            cosine_table,
            sine_table,
        )
        key_out = apply_rotary_embedding(
            root_mean_square_scale(key_in.reshape(tokens, kv_heads, head), key_scale),
            cosine_table,
            sine_table,
        )
        return (query_out, key_out)

    (query_rot, key_rot), heads_pull = jax.vjp(
        shape_heads, query_pre, key_pre, query_gain, key_norm_gain
    )

    def to_heads(value):
        return (
            value.reshape(p, micros, part, kv_heads, group, head)
            .transpose(1, 3, 4, 0, 2, 5)
            .reshape(micros, kv_heads, group, local_rows, head)
        )

    def from_heads(value):
        return (
            value.reshape(micros, kv_heads, group, p, part, head)
            .transpose(3, 0, 4, 1, 2, 5)
            .reshape(tokens, q_width)
        )

    query_low = to_heads(query_rot.astype(LOW))
    key_low = key_rot.astype(LOW).reshape(tokens, kv_width)

    def all_keys(slots):
        return (
            jnp.stack(slots)
            .reshape(n, p, micros, part, kv_heads, head)
            .transpose(2, 4, 0, 1, 3, 5)
            .reshape(micros, kv_heads, total_rows, head)
        )

    key_all = all_keys(gather_slots(key_low, "seq", go_a))
    value_all = all_keys(gather_slots(value_low, "seq", go_b))
    inside = jnp.concatenate(
        [(me_tp ^ k) * part + jnp.arange(part, dtype=jnp.int32) for k in range(p)]
    )
    query_pos = me_seq * local_rows + inside
    key_pos = jnp.concatenate([(me_seq ^ j) * local_rows + inside for j in range(n)])
    allowed = key_pos[None, :] <= query_pos[:, None]

    def all_scores():
        scores = (
            jnp.einsum("mngid,mnjd->mngij", query_low, key_all, preferred_element_type=F32) * scale
        )
        return jnp.where(allowed, scores, NEG_LARGE)

    scores = all_scores()
    peak = jnp.max(scores, axis=-1, keepdims=True)
    weights = jnp.exp(scores - peak)
    probability = weights / jnp.sum(weights, axis=-1, keepdims=True)
    probs_low = probability.astype(LOW)
    attended_heads = jnp.einsum("mngij,mnjd->mngid", probs_low, value_all, preferred_element_type=F32)
    attended = from_heads(attended_heads)
    gate_sig = jax.nn.sigmoid(gate_pre)
    gated_low = (attended * gate_sig).astype(LOW)
    branch = permute_columns(collect_tp(dot_nt(gated_low, w_o)))
    middle = x_part + branch
    normed_two = root_mean_square_scale(middle, second_gain).astype(LOW)
    n2 = jnp.concatenate(spread_tp(normed_two))

    gate_act = dot_nt(f_gate, n2)
    upward = dot_nt(f_up, n2)
    hidden_grad = dot_nt(f_down, cot)
    sig = jax.nn.sigmoid(gate_act)
    silu = gate_act * sig
    hidden_low = (silu * upward).astype(LOW)
    gate_grad = (hidden_grad * upward * sig * (1.0 + gate_act * (1.0 - sig))).astype(LOW)
    upward_grad = (hidden_grad * silu).astype(LOW)
    normed_two_grad = collect_tp(dot_tn(gate_grad, f_gate) + dot_tn(upward_grad, f_up))
    ffn_out = collect_tp(dot_tn(hidden_low, f_down))
    layer_rows = (middle + ffn_out).astype(LOW)
    d_gate = dot_nn(gate_grad, n2).astype(LOW).reshape(n, units, width)
    d_up = dot_nn(upward_grad, n2).astype(LOW).reshape(n, units, width)
    d_down = dot_nn(hidden_low, cot).astype(LOW).reshape(n, units, width)

    def return_units(own):
        result = jnp.zeros((p, units, chunk), F32)
        for k in range(p):
            piece = lax.dynamic_slice_in_dim(own, (me_tp ^ k) * chunk, chunk, 1)
            if k:
                piece = swap(piece.astype(LOW), "tp", k).astype(F32)
            result = lax.dynamic_update_slice_in_dim(result, piece[None], me_tp ^ k, 0)
        return result.reshape(p * units, chunk)

    grad_hgate = return_units(scatter_slots(list(d_gate), "seq", back_a)).T
    grad_hup = return_units(scatter_slots(list(d_up), "seq", back_b)).T
    grad_hdown = return_units(
        jnp.concatenate(
            [
                scatter_slots(list(d_down[:, :half]), "seq", back_a),
                scatter_slots(list(d_down[:, half:]), "seq", back_b),
            ]
        )
    )

    norm_two_pull = jax.vjp(root_mean_square_scale, middle, second_gain)[1]
    middle_from, grad_second = norm_two_pull(normed_two_grad)
    middle_grad = cot_part.astype(F32) + middle_from
    branch_grad = jnp.concatenate(spread_tp(permute_columns(middle_grad.astype(LOW))))
    gated_grad = dot_nn(branch_grad, w_o)
    attended_grad = (gated_grad * gate_sig).astype(LOW)
    gate_pre_grad = (gated_grad * attended * gate_sig * (1.0 - gate_sig)).astype(LOW)
    attended_grad_heads = to_heads(attended_grad)
    delta = jnp.sum(attended_grad_heads.astype(F32) * attended_heads, axis=-1, keepdims=True)
    probs_grad = jnp.einsum(
        "mngid,mnjd->mngij", attended_grad_heads, value_all, preferred_element_type=F32
    )
    scores_grad = (probability * (probs_grad - delta)).astype(LOW)
    query_grad = from_heads(
        jnp.einsum("mngij,mnjd->mngid", scores_grad, key_all, preferred_element_type=F32)
    )
    key_piece = jnp.einsum("mngij,mngid->mnjd", scores_grad, query_low, preferred_element_type=F32)
    value_piece = jnp.einsum(
        "mngij,mngid->mnjd", probs_low, attended_grad_heads, preferred_element_type=F32
    )

    def key_slots(value):
        return list(
            value.astype(LOW)
            .reshape(micros, kv_heads, n, p, part, head)
            .transpose(2, 3, 0, 4, 1, 5)
            .reshape(n, tokens, kv_width)
        )

    key_grad = scatter_slots(key_slots(key_piece), "seq", back_a)
    value_grad_low = scatter_slots(key_slots(value_piece), "seq", back_b).astype(LOW)
    query_pre_grad, key_pre_grad, grad_qgain, grad_kgain = heads_pull(
        (
            query_grad.reshape(tokens, q_heads, head) * scale,
            key_grad.reshape(tokens, kv_heads, head) * scale,
        )
    )
    query_pre_low = query_pre_grad.astype(LOW)
    kv_pre_low = jnp.concatenate([key_pre_grad.astype(LOW), value_grad_low], axis=1)

    def weight_grad(left, right, order):
        grad = dot_tn(left, right).astype(LOW)
        return scatter_slots(list(grad.reshape(n, block, right.shape[1])), "seq", order)

    grad_gating = weight_grad(normed, gate_pre_grad, back_a)
    grad_outproj = weight_grad(branch_grad, gated_low, back_b).T
    grad_query = weight_grad(normed, query_pre_low, back_a)
    grad_kv = weight_grad(normed, kv_pre_low, back_b)
    total = dot_nt(query_pre_low, w_q) + dot_nt(kv_pre_low, w_kv) + dot_nt(gate_pre_grad, w_g)
    normed_grad = permute_columns(collect_tp(total))
    norm_one_pull = jax.vjp(root_mean_square_scale, x_part, first_gain)[1]
    input_from, grad_first = norm_one_pull(normed_grad)
    input_grad = middle_grad + input_from

    gains = jnp.concatenate([grad_first, grad_second, grad_qgain, grad_kgain]).reshape(-1, head)
    gains = tree_sum(spread_tp(gains))
    for mask in masks:
        gains = gains + swap(gains, "seq", mask)
    gains = gains.reshape(-1)
    return (
        layer_rows.reshape(micros, part, width),
        input_grad.reshape(micros, part, width),
        gains[:width],
        grad_query,
        grad_kv[:, :kv_width],
        grad_kv[:, kv_width:],
        grad_gating,
        grad_outproj,
        gains[2 * width : 2 * width + head],
        gains[2 * width + head :],
        gains[width : 2 * width],
        grad_hgate,
        grad_hup,
        grad_hdown,
    )


def solution(mesh):
    in_specs = (
        P(None, "seq", None),
        P(None, "seq"),
        P(),
        P("seq", "tp"),
        P("seq", "tp"),
        P("seq", "tp"),
        P("seq", "tp"),
        P("tp", "seq"),
        P(),
        P(),
        P(),
        P("tp", "seq"),
        P("tp", "seq"),
        P("seq", "tp"),
        P(None, ("seq", "tp"), None),
    )
    out_specs = (
        P(None, ("seq", "tp"), None),
        P(None, ("seq", "tp"), None),
        P(),
        P("seq", "tp"),
        P("seq", "tp"),
        P("seq", "tp"),
        P("seq", "tp"),
        P("tp", "seq"),
        P(),
        P(),
        P(),
        P("tp", "seq"),
        P("tp", "seq"),
        P("seq", "tp"),
    )
    return jax.shard_map(
        per_device, mesh=mesh, in_specs=in_specs, out_specs=out_specs, check_vma=False
    )
```

time: 1670 us -> 768 us (0.46)
  waiting for transfers between devices: 1320 us -> 293 us
  local copies, waits for them, and re-layouts: 38.3 us -> 170 us
  starting transfers between devices: 1.93 us -> 132 us
  blocking collectives: 111 us -> 0 us
  matrix products: 108 us -> 61.5 us
  other arithmetic: 59 us -> 95.3 us
    reduce_scatter x22 -> x0, waiting for transfers between devices: 868 us -> none  [the longest x2 123 us: per_device(): lax.psum_scatter(ffn_grads[0].astype(jnp.bfloat16), 'tp', scatter_dimensi...]
    all_gather x12 -> x0, waiting for transfers between devices: 324 us -> none  [the longest x1 65 us: per_device(): lax.all_gather(hidden_down, 'tp', axis=1, tiled=True)]
    ppermute x0 -> x185, waiting for transfers between devices: none -> 293 us  [swap(): return lax.ppermute(value, axis, [(i, i ^ mask) for i in range(count)])]
    ppermute x0 -> x185, starting transfers between devices: none -> 132 us  [swap(): return lax.ppermute(value, axis, [(i, i ^ mask) for i in range(count)])]
    unnamed x39 -> x0, waiting for transfers between devices: 84.6 us -> none
    unnamed x268 -> x444, local copies, waits for them, and re-layouts: 21 us -> 104 us
    all_gather x6 -> x0, blocking collectives: 71.6 us -> none  [the longest x2 30.8 us: layer_pass(): lax.all_gather(middle_grad.astype(jnp.bfloat16), 'tp', axis=0, tiled=True)]
    dot_general x62 -> x26, matrix products: 108 us -> 58 us  [the longest x7 20.1 us: dot_nt(): lax.dot_general(left, right, (((1,), (1,)), ((), ())), preferred_element_...]
  transfers between devices with their start and end apart: 37 -> 185, of which waited for: 33 -> 58; matrix products, arithmetic and copies ran while one was open for 9% -> 40% of each run, Pallas kernels for 0% -> 0%
where the time goes in v1:
time: 768 us; the launch traced here: 756 us
  waiting for transfers between devices  293 us (38%)
  local copies, waits for them, and re-layouts  170 us (22%)
  starting transfers between devices  132 us (17%)
  other arithmetic  95.3 us (12%)
  matrix products  61.5 us (8%)
    ppermute x185, waiting for transfers between devices, swap(): return lax.ppermute(value, axis, [(i, i ^ mask) for i in range(count)])  293 us
    ppermute x185, starting transfers between devices, swap(): return lax.ppermute(value, axis, [(i, i ^ mask) for i in range(count)])  132 us
    unnamed x444, local copies, waits for them, and re-layouts  104 us
    convert_element_type x21, other arithmetic, scatter_slots(): now[s ^ mask].astype(LOW)  27.3 us
    dot_general x7, matrix products, dot_nt(): lax.dot_general(left, right, (((1,), (1,)), ((), ())), preferred_element_...  20.1 us
    dot_general x7, matrix products, dot_nn(): return jnp.dot(left, right, preferred_element_type=F32)  15.8 us
    dot_general x7, matrix products, dot_tn(): lax.dot_general(left, right, (((0,), (0,)), ((), ())), preferred_element_...  15.7 us
  transfers between devices with their start and end apart: 185, of which 58 were waited for; matrix products, arithmetic and copies ran while one was open for 40% of the time, Pallas kernels for 0%

profile of v1, /device:TPU:0, one launch (start us, length us, event | category | flops | bytes accessed | tf_op | source)
XLA Modules:
  0.0 756.0 jit_solution(9546082879609973219)
XLA Ops:
  47.6 6.9 collective-permute-done.70
  59.6 10.3 %collective-permute-done.59 = bf16[192,512]{1,0:T(8,128)(2,1)S(1)} collective-permute-done((bf16[192,512]{1,0:T(8,128)(2,1)S(1)}, bf16[192,512]{1,0:T(8,128)(2,1)S(1)}, u32[]{:S(2)}, u32[]{:S(2)}) %collective-permute-start.59) | collective-permute-done | bytes 196640 | tf_op jit(solution)/shard_map/ppermute | solution.py:49
  70.0 7.1 collective-permute-done.45
  78.8 10.2 %collective-permute-done.46 = bf16[192,512]{1,0:T(8,128)(2,1)S(1)} collective-permute-done((bf16[192,512]{1,0:T(8,128)(2,1)S(1)}, bf16[192,512]{1,0:T(8,128)(2,1)S(1)}, u32[]{:S(2)}, u32[]{:S(2)}) %collective-permute-start.46) | collective-permute-done | bytes 196640 | tf_op jit(solution)/shard_map/ppermute | solution.py:49
  106.9 4.8 collective-permute-done.29
  122.9 9.5 %collective-permute-done.5 = bf16[256,512]{1,0:T(8,128)(2,1)S(1)} collective-permute-done((bf16[256,512]{1,0:T(8,128)(2,1)}, bf16[256,512]{1,0:T(8,128)(2,1)S(1)}, u32[]{:S(2)}, u32[]{:S(2)}) %collective-permute-start.5) | collective-permute-done | bytes 262176 | tf_op jit(solution)/shard_map/ppermute | solution.py:49
  140.1 10.2 %collective-permute-done.12 = bf16[256,512]{1,0:T(8,128)(2,1)S(1)} collective-permute-done((bf16[256,512]{1,0:T(8,128)(2,1)S(1)}, bf16[256,512]{1,0:T(8,128)(2,1)S(1)}, u32[]{:S(2)}, u32[]{:S(2)}) %collective-permute-start.12) | collective-permute-done | bytes 262176 | tf_op jit(solution)/shard_map/ppermute | solution.py:49
  217.3 5.5 collective-permute-done.77
  222.8 7.4 collective-permute-done.78
  239.0 7.8 %collective-permute-done.81 = bf16[96,2048]{1,0:T(8,128)(2,1)} collective-permute-done((bf16[96,2048]{1,0:T(8,128)(2,1)}, bf16[96,2048]{1,0:T(8,128)(2,1)}, u32[]{:S(2)}, u32[]{:S(2)}) %collective-permute-start.81) | collective-permute-done | bytes 393248 | tf_op jit(solution)/shard_map/ppermute | solution.py:49
  250.1 5.1 collective-permute-done.49
  257.3 5.2 collective-permute-done.82
  271.5 4.7 collective-permute-done.26
  307.3 6.2 fusion.76
  313.5 4.4 collective-permute-done.64
  318.4 5.6 collective-permute-done.43
  346.1 7.1 collective-permute-done.53
  363.4 5.5 collective-permute-done.55
  369.0 4.9 fusion.94
  384.6 5.9 fusion.126
  416.7 5.5 collective-permute-done.96
  422.2 13.4 %collective-permute-done.95 = bf16[64,2048]{1,0:T(8,128)(2,1)S(1)} collective-permute-done((bf16[64,2048]{1,0:T(8,128)(2,1)S(1)}, bf16[64,2048]{1,0:T(8,128)(2,1)S(1)}, u32[]{:S(2)}, u32[]{:S(2)}) %collective-permute-start.95) | collective-permute-done | bytes 262176 | tf_op jit(solution)/shard_map/ppermute | solution.py:49
  546.5 23.7 %collective-permute-done.112 = bf16[64,2048]{1,0:T(8,128)(2,1)S(1)} collective-permute-done((bf16[64,2048]{1,0:T(8,128)(2,1)S(1)}, bf16[64,2048]{1,0:T(8,128)(2,1)S(1)}, u32[]{:S(2)}, u32[]{:S(2)}) %collective-permute-start.112) | collective-permute-done | bytes 262176 | tf_op jit(solution)/shard_map/ppermute | solution.py:49
  602.8 6.2 collective-permute-done.119
  613.1 5.0 collective-permute-done.147
  628.4 16.5 %collective-permute-done.136 = bf16[256,512]{1,0:T(8,128)(2,1)S(1)} collective-permute-done((bf16[256,512]{1,0:T(8,128)(2,1)}, bf16[256,512]{1,0:T(8,128)(2,1)S(1)}, u32[]{:S(2)}, u32[]{:S(2)}) %collective-permute-start.136) | collective-permute-done | bytes 262176 | tf_op jit(solution)/shard_map/ppermute | solution.py:49
  648.3 5.5 collective-permute-done.132
  658.6 8.1 %collective-permute-done.173 = bf16[96,2048]{1,0:T(8,128)(2,1)S(1)} collective-permute-done((bf16[96,2048]{1,0:T(8,128)(2,1)S(1)}, bf16[96,2048]{1,0:T(8,128)(2,1)S(1)}, u32[]{:S(2)}, u32[]{:S(2)}) %collective-permute-start.173) | collective-permute-done | bytes 393248 | tf_op jit(solution)/shard_map/ppermute | solution.py:49
  697.4 9.1 %collective-permute-done.183 = bf16[192,512]{1,0:T(8,128)(2,1)S(1)} collective-permute-done((bf16[192,512]{1,0:T(8,128)(2,1)S(1)}, bf16[192,512]{1,0:T(8,128)(2,1)S(1)}, u32[]{:S(2)}, u32[]{:S(2)}) %collective-permute-start.183) | collective-permute-done | bytes 196640 | tf_op jit(solution)/shard_map/ppermute | solution.py:49
  709.9 4.7 collective-permute-done.184
  727.2 5.5 collective-permute-done.164
  744.5 7.5 collective-permute-done.166
  (1027 shorter events, 507.1 us)
Async XLA Ops:
  0.7 99.2 %collective-permute-start = (bf16[256,512]{1,0:T(8,128)(2,1)}, bf16[256,512]{1,0:T(8,128)(2,1)}, u32[]{:S(2)}, u32[]{:S(2)}) collective-permute-start(bf16[256,512]{1,0:T(8,128)(2,1)} %param.18), channel_id=1, source_target_pairs={{0,4},{4,0},{8,12},{12,8},{16,20},{20,16},{24,28},{28,24},{1,5},{5... | collective-permute-start | bytes 786440 | tf_op jit(solution)/shard_map/ppermute | solution.py:49
  1.2 100.1 %collective-permute-start.1 = (bf16[256,512]{1,0:T(8,128)(2,1)}, bf16[256,512]{1,0:T(8,128)(2,1)}, u32[]{:S(2)}, u32[]{:S(2)}) collective-permute-start(bf16[256,512]{1,0:T(8,128)(2,1)} %param.18), channel_id=1, source_target_pairs={{0,8},{4,12},{8,0},{12,4},{16,24},{20,28},{24,16},{28,20},{1,9},{5... | collective-permute-start | bytes 786440 | tf_op jit(solution)/shard_map/ppermute | solution.py:49
  3.8 113.8 %collective-permute-start.3 = (bf16[256,512]{1,0:T(8,128)(2,1)}, bf16[256,512]{1,0:T(8,128)(2,1)}, u32[]{:S(2)}, u32[]{:S(2)}) collective-permute-start(bf16[256,512]{1,0:T(8,128)(2,1)} %param.18), channel_id=1, source_target_pairs={{0,16},{4,20},{8,24},{12,28},{16,0},{20,4},{24,8},{28,12},{1,17},{... | collective-permute-start | bytes 786440 | tf_op jit(solution)/shard_map/ppermute | solution.py:49
  7.2 37.5 %collective-permute-start.68 = (bf16[192,512]{1,0:T(8,128)(2,1)}, bf16[192,512]{1,0:T(8,128)(2,1)}, u32[]{:S(2)}, u32[]{:S(2)}) collective-permute-start(bf16[192,512]{1,0:T(8,128)(2,1)} %get-tuple-element.235), channel_id=1, source_target_pairs={{0,1},{1,0},{2,3},{3,2},{4,5},{5,4},{6,7},{7,6},{8,9},{9,8},{10,11... | collective-permute-start | bytes 589832 | tf_op jit(solution)/shard_map/ppermute | solution.py:49
  8.8 37.1 %collective-permute-start.69 = (bf16[192,512]{1,0:T(8,128)(2,1)}, bf16[192,512]{1,0:T(8,128)(2,1)}, u32[]{:S(2)}, u32[]{:S(2)}) collective-permute-start(bf16[192,512]{1,0:T(8,128)(2,1)} %get-tuple-element.234), channel_id=1, source_target_pairs={{0,2},{1,3},{2,0},{3,1},{4,6},{5,7},{6,4},{7,5},{8,10},{9,11},{10,... | collective-permute-start | bytes 589832 | tf_op jit(solution)/shard_map/ppermute | solution.py:49
  69.9 32.5 %collective-permute-start.7 = (bf16[256,512]{1,0:T(8,128)(2,1)S(1)}, bf16[256,512]{1,0:T(8,128)(2,1)S(1)}, u32[]{:S(2)}, u32[]{:S(2)}) collective-permute-start(bf16[256,512]{1,0:T(8,128)(2,1)S(1)} %copy-done.111), channel_id=1, source_target_pairs={{0,4},{4,0},{8,12},{12,8},{16,20},{20,16},{24,28},{28,24},{1,5},{5... | collective-permute-start | bytes 786440 | tf_op jit(solution)/shard_map/ppermute | solution.py:49
  132.4 29.7 %collective-permute-start.71 = (bf16[96,2048]{1,0:T(8,128)(2,1)S(1)}, bf16[96,2048]{1,0:T(8,128)(2,1)S(1)}, u32[]{:S(2)}, u32[]{:S(2)}) collective-permute-start(bf16[96,2048]{1,0:T(8,128)(2,1)S(1)} %get-tuple-element.232), channel_id=1, source_target_pairs={{0,4},{4,0},{8,12},{12,8},{16,20},{20,16},{24,28},{28,24},{1,5},{5... | collective-permute-start | bytes 1179656 | tf_op jit(solution)/shard_map/ppermute | solution.py:49
  133.7 30.5 %collective-permute-start.73 = (bf16[96,2048]{1,0:T(8,128)(2,1)S(1)}, bf16[96,2048]{1,0:T(8,128)(2,1)}, u32[]{:S(2)}, u32[]{:S(2)}) collective-permute-start(bf16[96,2048]{1,0:T(8,128)(2,1)S(1)} %get-tuple-element.232), channel_id=1, source_target_pairs={{0,8},{4,12},{8,0},{12,4},{16,24},{20,28},{24,16},{28,20},{1,9},{5... | collective-permute-start | bytes 1179656 | tf_op jit(solution)/shard_map/ppermute | solution.py:49
  160.4 54.8 %collective-permute-start.61 = (bf16[192,2048]{1,0:T(8,128)(2,1)S(1)}, bf16[192,2048]{1,0:T(8,128)(2,1)}, u32[]{:S(2)}, u32[]{:S(2)}) collective-permute-start(bf16[192,2048]{1,0:T(8,128)(2,1)S(1)} %constant_dynamic-update-slice_fusion.145), channel_id=1, source_target_pairs={{0,4},{4,0},{8,12},{12,8},{16,20},{20,16},{24,28},{28,24},{1,5},{5... | collective-permute-start | bytes 2359304 | tf_op jit(solution)/shard_map/ppermute | solution.py:49
  169.0 41.5 %collective-permute-start.75 = (bf16[96,2048]{1,0:T(8,128)(2,1)}, bf16[96,2048]{1,0:T(8,128)(2,1)}, u32[]{:S(2)}, u32[]{:S(2)}) collective-permute-start(bf16[96,2048]{1,0:T(8,128)(2,1)} %collective-permute-done.73), channel_id=1, source_target_pairs={{0,4},{4,0},{8,12},{12,8},{16,20},{20,16},{24,28},{28,24},{1,5},{5... | collective-permute-start | bytes 1179656 | tf_op jit(solution)/shard_map/ppermute | solution.py:49
  205.8 97.1 %collective-permute-start.90 = (bf16[64,2048]{1,0:T(8,128)(2,1)}, bf16[64,2048]{1,0:T(8,128)(2,1)}, u32[]{:S(2)}, u32[]{:S(2)}) collective-permute-start(bf16[64,2048]{1,0:T(8,128)(2,1)} %bitcast.56), channel_id=1, source_target_pairs={{0,3},{1,2},{2,1},{3,0},{4,7},{5,6},{6,5},{7,4},{8,11},{9,10},{10,... | collective-permute-start | bytes 786440 | tf_op jit(solution)/shard_map/ppermute | solution.py:49
  215.2 89.7 %collective-permute-start.89 = (bf16[64,2048]{1,0:T(8,128)(2,1)}, bf16[64,2048]{1,0:T(8,128)(2,1)}, u32[]{:S(2)}, u32[]{:S(2)}) collective-permute-start(bf16[64,2048]{1,0:T(8,128)(2,1)} %bitcast.56), channel_id=1, source_target_pairs={{0,2},{1,3},{2,0},{3,1},{4,6},{5,7},{6,4},{7,5},{8,10},{9,11},{10,... | collective-permute-start | bytes 786440 | tf_op jit(solution)/shard_map/ppermute | solution.py:49
  238.0 66.8 %collective-permute-start.88 = (bf16[64,2048]{1,0:T(8,128)(2,1)}, bf16[64,2048]{1,0:T(8,128)(2,1)}, u32[]{:S(2)}, u32[]{:S(2)}) collective-permute-start(bf16[64,2048]{1,0:T(8,128)(2,1)} %bitcast.56), channel_id=1, source_target_pairs={{0,1},{1,0},{2,3},{3,2},{4,5},{5,4},{6,7},{7,6},{8,9},{9,8},{10,11... | collective-permute-start | bytes 786440 | tf_op jit(solution)/shard_map/ppermute | solution.py:49
  300.6 33.5 %collective-permute-start.51 = (bf16[192,2048]{1,0:T(8,128)(2,1)}, bf16[192,2048]{1,0:T(8,128)(2,1)}, u32[]{:S(2)}, u32[]{:S(2)}) collective-permute-start(bf16[192,2048]{1,0:T(8,128)(2,1)} %constant_dynamic-update-slice_fusion.148), channel_id=1, source_target_pairs={{0,16},{4,20},{8,24},{12,28},{16,0},{20,4},{24,8},{28,12},{1,17},{... | collective-permute-start | bytes 2359304 | tf_op jit(solution)/shard_map/ppermute | solution.py:49
  396.4 87.5 %collective-permute-start.149 = (bf16[192,2048]{1,0:T(8,128)(2,1)}, bf16[192,2048]{1,0:T(8,128)(2,1)}, u32[]{:S(2)}, u32[]{:S(2)}) collective-permute-start(bf16[192,2048]{1,0:T(8,128)(2,1)} %get-tuple-element.158), channel_id=1, source_target_pairs={{0,4},{4,0},{8,12},{12,8},{16,20},{20,16},{24,28},{28,24},{1,5},{5... | collective-permute-start | bytes 2359304 | tf_op jit(solution)/shard_map/ppermute | solution.py:49
  396.4 88.1 %collective-permute-start.152 = (bf16[192,2048]{1,0:T(8,128)(2,1)}, bf16[192,2048]{1,0:T(8,128)(2,1)}, u32[]{:S(2)}, u32[]{:S(2)}) collective-permute-start(bf16[192,2048]{1,0:T(8,128)(2,1)} %get-tuple-element.156), channel_id=1, source_target_pairs={{0,4},{4,0},{8,12},{12,8},{16,20},{20,16},{24,28},{28,24},{1,5},{5... | collective-permute-start | bytes 2359304 | tf_op jit(solution)/shard_map/ppermute | solution.py:49
  422.2 66.1 %collective-permute-start.159 = (bf16[192,2048]{1,0:T(8,128)(2,1)}, bf16[192,2048]{1,0:T(8,128)(2,1)}, u32[]{:S(2)}, u32[]{:S(2)}) collective-permute-start(bf16[192,2048]{1,0:T(8,128)(2,1)} %get-tuple-element.152), channel_id=1, source_target_pairs={{0,4},{4,0},{8,12},{12,8},{16,20},{20,16},{24,28},{28,24},{1,5},{5... | collective-permute-start | bytes 2359304 | tf_op jit(solution)/shard_map/ppermute | solution.py:49
  435.7 53.1 %collective-permute-start.162 = (bf16[192,2048]{1,0:T(8,128)(2,1)}, bf16[192,2048]{1,0:T(8,128)(2,1)}, u32[]{:S(2)}, u32[]{:S(2)}) collective-permute-start(bf16[192,2048]{1,0:T(8,128)(2,1)} %get-tuple-element.150), channel_id=1, source_target_pairs={{0,4},{4,0},{8,12},{12,8},{16,20},{20,16},{24,28},{28,24},{1,5},{5... | collective-permute-start | bytes 2359304 | tf_op jit(solution)/shard_map/ppermute | solution.py:49
  502.7 35.6 %collective-permute-start.123 = (bf16[256,512]{1,0:T(8,128)(2,1)}, bf16[256,512]{1,0:T(8,128)(2,1)}, u32[]{:S(2)}, u32[]{:S(2)}) collective-permute-start(bf16[256,512]{1,0:T(8,128)(2,1)} %get-tuple-element.184), channel_id=1, source_target_pairs={{0,4},{4,0},{8,12},{12,8},{16,20},{20,16},{24,28},{28,24},{1,5},{5... | collective-permute-start | bytes 786440 | tf_op jit(solution)/shard_map/ppermute | solution.py:49
  512.5 30.1 %collective-permute-start.137 = (bf16[256,512]{1,0:T(8,128)(2,1)}, bf16[256,512]{1,0:T(8,128)(2,1)}, u32[]{:S(2)}, u32[]{:S(2)}) collective-permute-start(bf16[256,512]{1,0:T(8,128)(2,1)} %get-tuple-element.172), channel_id=1, source_target_pairs={{0,4},{4,0},{8,12},{12,8},{16,20},{20,16},{24,28},{28,24},{1,5},{5... | collective-permute-start | bytes 786440 | tf_op jit(solution)/shard_map/ppermute | solution.py:49
  538.3 31.9 %collective-permute-start.112 = (bf16[64,2048]{1,0:T(8,128)(2,1)S(1)}, bf16[64,2048]{1,0:T(8,128)(2,1)S(1)}, u32[]{:S(2)}, u32[]{:S(2)}) collective-permute-start(bf16[64,2048]{1,0:T(8,128)(2,1)S(1)} %get-tuple-element.199), channel_id=1, source_target_pairs={{0,2},{1,3},{2,0},{3,1},{4,6},{5,7},{6,4},{7,5},{8,10},{9,11},{10,... | collective-permute-start | bytes 786440 | tf_op jit(solution)/shard_map/ppermute | solution.py:49
  538.3 32.4 %collective-permute-start.111 = (bf16[64,2048]{1,0:T(8,128)(2,1)S(1)}, bf16[64,2048]{1,0:T(8,128)(2,1)S(1)}, u32[]{:S(2)}, u32[]{:S(2)}) collective-permute-start(bf16[64,2048]{1,0:T(8,128)(2,1)S(1)} %get-tuple-element.197), channel_id=1, source_target_pairs={{0,1},{1,0},{2,3},{3,2},{4,5},{5,4},{6,7},{7,6},{8,9},{9,8},{10,11... | collective-permute-start | bytes 786440 | tf_op jit(solution)/shard_map/ppermute | solution.py:49
  542.6 41.0 %collective-permute-start.87 = (bf16[64,2048]{1,0:T(8,128)(2,1)}, bf16[64,2048]{1,0:T(8,128)(2,1)S(1)}, u32[]{:S(2)}, u32[]{:S(2)}) collective-permute-start(bf16[64,2048]{1,0:T(8,128)(2,1)} %get-tuple-element.222), channel_id=1, source_target_pairs={{0,3},{1,2},{2,1},{3,0},{4,7},{5,6},{6,5},{7,4},{8,11},{9,10},{10,... | collective-permute-start | bytes 786440 | tf_op jit(solution)/shard_map/ppermute | solution.py:49
  544.5 39.2 %collective-permute-start.86 = (bf16[64,2048]{1,0:T(8,128)(2,1)}, bf16[64,2048]{1,0:T(8,128)(2,1)S(1)}, u32[]{:S(2)}, u32[]{:S(2)}) collective-permute-start(bf16[64,2048]{1,0:T(8,128)(2,1)} %get-tuple-element.223), channel_id=1, source_target_pairs={{0,2},{1,3},{2,0},{3,1},{4,6},{5,7},{6,4},{7,5},{8,10},{9,11},{10,... | collective-permute-start | bytes 786440 | tf_op jit(solution)/shard_map/ppermute | solution.py:49
  591.4 62.5 %collective-permute-start.151 = (bf16[192,2048]{1,0:T(8,128)(2,1)}, bf16[192,2048]{1,0:T(8,128)(2,1)}, u32[]{:S(2)}, u32[]{:S(2)}) collective-permute-start(bf16[192,2048]{1,0:T(8,128)(2,1)} %get-tuple-element.157), channel_id=1, source_target_pairs={{0,4},{4,0},{8,12},{12,8},{16,20},{20,16},{24,28},{28,24},{1,5},{5... | collective-permute-start | bytes 2359304 | tf_op jit(solution)/shard_map/ppermute | solution.py:49
  591.5 30.1 %collective-permute-start.120 = (bf16[256,512]{1,0:T(8,128)(2,1)}, bf16[256,512]{1,0:T(8,128)(2,1)}, u32[]{:S(2)}, u32[]{:S(2)}) collective-permute-start(bf16[256,512]{1,0:T(8,128)(2,1)} %get-tuple-element.182), channel_id=1, source_target_pairs={{0,4},{4,0},{8,12},{12,8},{16,20},{20,16},{24,28},{28,24},{1,5},{5... | collective-permute-start | bytes 786440 | tf_op jit(solution)/shard_map/ppermute | solution.py:49
  612.1 43.3 %collective-permute-start.153 = (bf16[192,2048]{1,0:T(8,128)(2,1)}, bf16[192,2048]{1,0:T(8,128)(2,1)}, u32[]{:S(2)}, u32[]{:S(2)}) collective-permute-start(bf16[192,2048]{1,0:T(8,128)(2,1)} %get-tuple-element.160), channel_id=1, source_target_pairs={{0,8},{4,12},{8,0},{12,4},{16,24},{20,28},{24,16},{28,20},{1,9},{5... | collective-permute-start | bytes 2359304 | tf_op jit(solution)/shard_map/ppermute | solution.py:49
  628.4 40.1 %collective-permute-start.161 = (bf16[192,2048]{1,0:T(8,128)(2,1)}, bf16[192,2048]{1,0:T(8,128)(2,1)S(1)}, u32[]{:S(2)}, u32[]{:S(2)}) collective-permute-start(bf16[192,2048]{1,0:T(8,128)(2,1)} %get-tuple-element.151), channel_id=1, source_target_pairs={{0,4},{4,0},{8,12},{12,8},{16,20},{20,16},{24,28},{28,24},{1,5},{5... | collective-permute-start | bytes 2359304 | tf_op jit(solution)/shard_map/ppermute | solution.py:49
  653.8 30.7 %collective-permute-start.168 = (bf16[96,2048]{1,0:T(8,128)(2,1)S(1)}, bf16[96,2048]{1,0:T(8,128)(2,1)S(1)}, u32[]{:S(2)}, u32[]{:S(2)}) collective-permute-start(bf16[96,2048]{1,0:T(8,128)(2,1)S(1)} %copy-done.62), channel_id=1, source_target_pairs={{0,4},{4,0},{8,12},{12,8},{16,20},{20,16},{24,28},{28,24},{1,5},{5... | collective-permute-start | bytes 1179656 | tf_op jit(solution)/shard_map/ppermute | solution.py:49
  684.4 37.1 %collective-permute-start.158 = (bf16[192,2048]{1,0:T(8,128)(2,1)S(1)}, bf16[192,2048]{1,0:T(8,128)(2,1)S(1)}, u32[]{:S(2)}, u32[]{:S(2)}) collective-permute-start(bf16[192,2048]{1,0:T(8,128)(2,1)S(1)} %copy-done.51), channel_id=1, source_target_pairs={{0,4},{4,0},{8,12},{12,8},{16,20},{20,16},{24,28},{28,24},{1,5},{5... | collective-permute-start | bytes 2359304 | tf_op jit(solution)/shard_map/ppermute | solution.py:49
  684.6 31.2 %collective-permute-start.150 = (bf16[192,2048]{1,0:T(8,128)(2,1)S(1)}, bf16[192,2048]{1,0:T(8,128)(2,1)S(1)}, u32[]{:S(2)}, u32[]{:S(2)}) collective-permute-start(bf16[192,2048]{1,0:T(8,128)(2,1)S(1)} %copy-done.54), channel_id=1, source_target_pairs={{0,8},{4,12},{8,0},{12,4},{16,24},{20,28},{24,16},{28,20},{1,9},{5... | collective-permute-start | bytes 2359304 | tf_op jit(solution)/shard_map/ppermute | solution.py:49
  685.7 31.3 %collective-permute-start.154 = (bf16[192,2048]{1,0:T(8,128)(2,1)S(1)}, bf16[192,2048]{1,0:T(8,128)(2,1)S(1)}, u32[]{:S(2)}, u32[]{:S(2)}) collective-permute-start(bf16[192,2048]{1,0:T(8,128)(2,1)S(1)} %add_convert_fusion.3), channel_id=1, source_target_pairs={{0,16},{4,20},{8,24},{12,28},{16,0},{20,4},{24,8},{28,12},{1,17},{... | collective-permute-start | bytes 2359304 | tf_op jit(solution)/shard_map/ppermute | solution.py:49
  (309 other events, 3804.4 us)
